TPU v7x, 768 devices: a whole 4x8x12 slice. The times are simulated.
768 devices in a mesh: fsdp: 48 (over y_lo, z, core), frame: 16 (over x, y_hi).
Axes of the slice: x: 4, y: 8 (y_hi: 4, y_lo: 2; y = y_hi * 2 + y_lo), z: 12, core: 2. Of those that a mesh axis runs over, the one named last changes fastest.
Arguments:
- frames: bfloat16 [48, 6144, 3072], P('fsdp', 'frame'), may hold values from -6 to 6
- modulation: float32 [48, 2, 3072], P('fsdp'), may hold values from -3 to 3
- w_qkv: bfloat16 [3072, 768], P('fsdp'), may hold values from -0.109375 to 0.109375
- qk_gain: float32 [2, 128], replicated, may hold values from 0.1 to 1.9
- w_out: bfloat16 [256, 3072], P(None, 'fsdp'), may hold values from -0.375 to 0.375
Outputs:
- mixed: bfloat16 [48, 6144, 3072], P('fsdp', 'frame')
All inputs are finite; a program needn't handle non-finite values.
Results may differ from a plain program's by a relative error of at most 0.0053.
Values may be sent and summed in bfloat16 or wider, within the bound.
A program may use at most 64 MiB of HBM per device.

v0:
```python
import math

import jax
import jax.numpy as jnp
from jax import lax
from jax.sharding import Mesh
from jax.sharding import PartitionSpec as P

D = 3072
HEAD_DIM = 128
HEADS = 2
TILE = 128
REACH = 2
BORDER = 256
WINDOW = 640
FSDP = ("fsdp_0", "fsdp_1", "fsdp_2")


def with_halo(cells, sides, width):
    for axis, dim in sides:
        count = lax.axis_size(axis)
        ends = count - 1
        head = lax.slice_in_dim(cells, 0, width, axis=dim)
        tail = lax.slice_in_dim(cells, cells.shape[dim] - width, cells.shape[dim], axis=dim)
        cells = jnp.concatenate(
            [
                lax.ppermute(tail, axis, [(i, (i + 1) % count) for i in range(ends)]),
                cells,
                lax.ppermute(head, axis, [((i + 1) % count, i) for i in range(ends)]),
            ],
            axis=dim,
        )
    return cells


def joined_along(parts, dim):
    parts = jnp.moveaxis(parts, 0, dim)
    shape = parts.shape
    return parts.reshape(*shape[:dim], shape[dim] * shape[dim + 1], *shape[dim + 2 :])


def all_blocks(array, axes, sequence):
    parts = array[None]
    for k in sequence:
        parts = lax.all_gather(parts, axes[k], axis=0, tiled=True)
    block = [lax.axis_size(axes[k]) for k in reversed(sequence)]
    parts = parts.reshape(*block, *array.shape)
    turned = sorted(range(len(sequence)), key=lambda place: sequence[len(sequence) - 1 - place])
    return parts.transpose(*turned, *range(len(sequence), parts.ndim)).reshape(-1, *array.shape)


def gathered_by_axis(array, axes, sequence, dim):
    return joined_along(all_blocks(array, axes, sequence), dim)


def norm_rows(frames_rows, modulation_rows):
    values_full = frames_rows.astype(jnp.float32)
    average = jnp.mean(values_full, axis=-1, keepdims=True)
    centered = values_full - average
    spread = jnp.mean(centered * centered, axis=-1, keepdims=True)
    normed = centered * lax.rsqrt(spread + 1e-06)
    return (normed * (1.0 + modulation_rows[0]) + modulation_rows[1]).astype(jnp.bfloat16)


def head_norm(projected, gain_row):
    count = projected.shape[0]
    shaped = projected.reshape(count, HEADS, HEAD_DIM)
    squares = jnp.mean(shaped * shaped, axis=-1, keepdims=True)
    scaled = shaped * lax.rsqrt(squares + 1e-06) * gain_row
    return scaled.reshape(count, HEADS * HEAD_DIM).astype(jnp.bfloat16)


def send_borders(key_part, value_part):
    stacked = jnp.concatenate([key_part, value_part], axis=1)
    return with_halo(stacked, (("frame", 0),), BORDER)


def make_folder(normed, proj_width):

    def fold_rows(carry, block_rows, first_row):
        running = jnp.dot(normed, block_rows[:, :proj_width], preferred_element_type=jnp.float32)
        stashed = block_rows[:, proj_width:]
        return (running, stashed)

    return fold_rows


def on_device(frames, modulation, w_qkv, qk_gain, w_out):
    normed = norm_rows(frames[0], modulation[0])
    rows_here = normed.shape[0]
    width = HEADS * HEAD_DIM
    scale_factor = 1.0 / math.sqrt(HEAD_DIM)
    out_rows_t = jnp.transpose(w_out)
    stash_init = jnp.zeros((D, width), jnp.bfloat16)
    proj_width = w_qkv.shape[1]
    zeros_init = jnp.zeros((rows_here, proj_width), jnp.float32)
    folder = make_folder(normed, proj_width)
    operand, folder, start_carry = (
        jnp.concatenate([w_qkv, out_rows_t], axis=1),
        folder,
        (zeros_init, stash_init),
    )
    result = folder(start_carry, gathered_by_axis(operand, FSDP, (0, 1, 2), 0), jnp.int32(0))
    projected = result[0]
    stashed = result[1]
    queries = head_norm(projected[:, :width], qk_gain[0])
    key_part = head_norm(projected[:, width : 2 * width], qk_gain[1])
    value_part = projected[:, 2 * width :].astype(jnp.bfloat16)
    padded = send_borders(key_part, value_part)
    tiles_here = rows_here // TILE
    video_tokens = rows_here * lax.axis_size("frame")
    tile_ids = jnp.arange(tiles_here, dtype=jnp.int32)
    first_tile = tile_ids - REACH
    pieces = []
    for offset in range(2 * REACH + 1):
        pieces.append(
            padded[offset * TILE : offset * TILE + rows_here].reshape(tiles_here, TILE, 2 * width)
        )
    windows = jnp.concatenate(pieces, axis=1)
    positions = (
        lax.axis_index("frame") * rows_here
        + first_tile[:, None] * TILE
        + jnp.arange(WINDOW, dtype=jnp.int32)[None, :]
    )
    inside = (positions >= 0) & (positions < video_tokens)
    key_win = windows[:, :, :width].reshape(tiles_here, WINDOW, HEADS, HEAD_DIM)
    value_win = windows[:, :, width:].reshape(tiles_here, WINDOW, HEADS, HEAD_DIM)
    query_tiles = queries.reshape(tiles_here, TILE, HEADS, HEAD_DIM)
    scores = (
        jnp.einsum("tqhd,tkhd->thqk", query_tiles, key_win, preferred_element_type=jnp.float32)
        * scale_factor
    )
    raised = jnp.where(inside[:, None, None, :], jnp.exp(scores), 0.0)
    probs = (raised / jnp.sum(raised, axis=-1, keepdims=True)).astype(jnp.bfloat16)
    attended = jnp.einsum("thqk,tkhd->tqhd", probs, value_win, preferred_element_type=jnp.float32)
    attended = attended.astype(jnp.bfloat16).reshape(rows_here, width)
    mixed = lax.dot_general(
        attended, stashed, (((1,), (1,)), ((), ())), preferred_element_type=jnp.float32
    ).astype(jnp.bfloat16)
    return mixed[None]


def solution(mesh):
    finer = Mesh(
        mesh.devices.reshape(2, 12, 2, mesh.shape["frame"]), ("fsdp_0", "fsdp_1", "fsdp_2", "frame")
    )
    placed = (P(FSDP, "frame", None), P(FSDP, None, None), P(FSDP, None), P(), P(None, FSDP))
    return jax.shard_map(
        on_device, mesh=finer, in_specs=placed, out_specs=P(FSDP, "frame", None), check_vma=False
    )
```

profile of v0, /device:TPU:1, one launch (start us, length us, event | category | flops | bytes accessed | tf_op | source)
XLA Modules:
  0.0 163.8 jit_solution(5075813596218256460)
XLA Ops:
  6.5 0.0 all-gather.4.cloned.1.call-start
  6.5 0.9 pad_maximum_fusion.2
  7.5 0.0 copy-start.9
  7.5 0.0 copy-start.1
  7.5 5.4 %all-gather = bf16[128,1024]{1,0:T(8,128)(2,1)} all-gather(bf16[64,1024]{1,0:T(8,128)(2,1)S(1)} %pad_maximum_fusion.2), channel_id=2, replica_groups=mesh['fsdp_0'=2,'fsdp_1'=12,'fsdp_2'=2,'frame'=16] {'fsdp_0'}, dimensions={0}, use_global_device_ids=true | all-gather | bytes 393216 | tf_op jit(solution)/shard_map/all_gather | solution.py:45
  12.9 0.0 all-gather.4.cloned.1.call-update
  12.9 0.0 all-gather.6.cloned.1.call-start
  12.9 65.1 %all-gather.4.cloned.1.call-done = bf16[24,64,1024]{2,1,0:T(8,128)(2,1)} async-done(((bf16[2,64,1024]{2,1,0:T(8,128)(2,1)}), bf16[24,64,1024]{2,1,0:T(8,128)(2,1)}) %all-gather.4.cloned.1.call-update) | async-done | bytes 3145744 | tf_op jit(solution)/shard_map/all_gather | solution.py:45
  78.0 0.0 all-gather.6.cloned.1.call-update
  78.0 0.5 multiply_add_fusion
  78.6 0.0 copy-done.9
  78.6 0.6 broadcast_bitcast_fusion
  79.2 0.0 copy-done.1
  79.2 0.4 convert_reduce_fusion
  79.6 0.8 fusion.3
  80.3 0.6 add_rsqrt_fusion.2
  80.9 0.0 copy-done.4
  80.9 0.6 slice_add_fusion
  81.5 32.9 %all-gather.6.cloned.1.call-done = bf16[48,64,1024]{2,1,0:T(8,128)(2,1)} async-done(((bf16[24,64,1024]{2,1,0:T(8,128)(2,1)}), bf16[48,64,1024]{2,1,0:T(8,128)(2,1)}) %all-gather.6.cloned.1.call-update) | async-done | bytes 6291472 | tf_op jit(solution)/shard_map/all_gather | solution.py:45
  114.5 3.5 %copy.45 = bf16[2,12,2,64,1024]{4,3,2,1,0:T(8,128)(2,1)S(1)} copy(bf16[2,12,2,64,1024]{4,3,0,1,2:T(8,128)(2,1)} %bitcast.67) | data formatting | bytes 12582912 | tf_op jit(solution)/shard_map/transpose | solution.py:49
  118.0 0.0 copy-start
  118.0 0.0 copy-done.5
  118.0 0.0 copy-done.8
  118.0 2.4 %fusion.7 = f32[384,768]{1,0:T(8,128)S(1)} fusion(bf16[3072,1024]{1,0:T(8,128)(2,1)S(1)} %bitcast.65, bf16[1,384,3072]{2,1,0:T(8,128)(2,1)S(1)} %copy-done.1, f32[3072]{0:T(1024)S(1)} %bitcast.81, f32[3072]{0:T(1024)S(1)} %bitcast.80, f32[384]{0:T(512)S(1)} %copy-done.8, f32[384]{0:T(512)S(1)} %broadcast_multiply_fusion), kind=kOutput, calls=%fused_computation.9 | convolution fusion | flops 1819017216 | bytes 8286208 | tf_op jit(solution)/shard_map/dot_general | solution.py:81
  120.4 0.2 copy-done
  120.7 0.1 slice_multiply_fusion
  120.7 0.2 mul.106
  120.9 0.0 copy-start.6
  121.0 0.0 copy-start.7
  121.0 0.5 reduce_sum.47
  121.5 0.2 mul.118
  121.7 0.5 reduce_sum.48
  122.2 0.0 copy-start.10
  122.2 0.5 mul.107
  122.7 0.5 mul.119
  123.2 0.0 copy-done.6
  123.2 0.0 copy-done.7
  123.2 0.1 fusion.20
  123.4 2.3 %collective-permute-start = (bf16[256,512]{1,0:T(8,128)(2,1)S(1)}, bf16[256,512]{1,0:T(8,128)(2,1)S(1)}, u32[]{:S(2)}, u32[]{:S(2)}) collective-permute-start(bf16[256,512]{1,0:T(8,128)(2,1)S(1)} %get-tuple-element.18), channel_id=1, source_target_pairs={{0,1},{1,2},{2,3},{3,4},{4,5},{5,6},{6,7},{7,8},{8,9},{9,10},{10,1... | collective-permute-start | bytes 786440 | tf_op jit(solution)/shard_map/ppermute | solution.py:27
  125.7 1.3 collective-permute-start.1
  127.0 0.1 fusion.31
  127.1 0.2 copy.50
  127.3 0.7 reshape.118
  128.1 5.0 %collective-permute-done = bf16[256,512]{1,0:T(8,128)(2,1)S(1)} collective-permute-done((bf16[256,512]{1,0:T(8,128)(2,1)S(1)}, bf16[256,512]{1,0:T(8,128)(2,1)S(1)}, u32[]{:S(2)}, u32[]{:S(2)}) %collective-permute-start) | collective-permute-done | bytes 262176 | tf_op jit(solution)/shard_map/ppermute | solution.py:27
  133.1 10.2 %collective-permute-done.1 = bf16[256,512]{1,0:T(8,128)(2,1)S(1)} collective-permute-done((bf16[256,512]{1,0:T(8,128)(2,1)S(1)}, bf16[256,512]{1,0:T(8,128)(2,1)S(1)}, u32[]{:S(2)}, u32[]{:S(2)}) %collective-permute-start.1) | collective-permute-done | bytes 262176 | tf_op jit(solution)/shard_map/ppermute | solution.py:29
  143.3 0.1 pad_maximum_fusion
  143.4 0.8 fusion.36
  144.2 0.2 copy.48
  144.4 0.1 constant_dynamic-update-slice_fusion.4
  144.5 1.2 copy.49
  145.7 0.9 fusion.35
  146.6 1.2 copy.51
  147.9 1.9 %copy.52 = bf16[3,128,512]{1,2,0:T(8,128)(2,1)} copy(bf16[3,128,512]{2,1,0:T(8,128)(2,1)} %bitcast.73) | data formatting | bytes 786432 | tf_op jit(solution)/shard_map/reshape | solution.py:117
  149.8 0.1 constant_dynamic-update-slice_fusion.3
  149.9 0.1 constant_dynamic-update-slice_fusion.2
  150.0 0.1 constant_dynamic-update-slice_fusion.1
  150.1 0.7 copy-done.2
  150.8 0.1 constant_dynamic-update-slice_fusion
  150.9 0.2 fusion.34
  151.1 0.7 copy-done.3
  151.8 0.7 fusion.15
  152.5 0.7 fusion.17
  153.2 0.2 copy.57
  153.3 3.6 %fusion.9 = bf16[1,384,3072]{2,1,0:T(8,128)(2,1)} fusion(bf16[3072,1024]{1,0:T(8,128)(2,1)} %bitcast.66, bf16[48,8,2,128]{3,2,1,0:T(2,128)(2,1)S(1)} %bitcast.78), kind=kOutput, calls=%fused_computation.12 | convolution fusion | flops 605159424 | bytes 4128768 | tf_op jit(solution)/shard_map/dot_general | solution.py:137
  (13 shorter events, 0.2 us)
Async XLA Ops:
  6.5 71.5 %all-gather.4.cloned.1.call-start = ((), (), s32[]{:S(2)}) async-start(), calls=%async_computation | async-start | bytes 3407872 | tf_op jit(solution)/shard_map/all_gather | solution.py:45
  7.5 71.1 %copy-start.9 = (f32[2,128]{1,0:T(2,128)S(1)}, f32[2,128]{1,0:T(2,128)}, u32[]{:S(2)}) copy-start(f32[2,128]{1,0:T(2,128)} %param.8) | copy-start | bytes 3076
  7.5 71.7 %copy-start.1 = (bf16[1,384,3072]{2,1,0:T(8,128)(2,1)S(1)}, bf16[1,384,3072]{2,1,0:T(8,128)(2,1)}, u32[]{:S(2)}) copy-start(bf16[1,384,3072]{2,1,0:T(8,128)(2,1)} %param.5) | copy-start | bytes 7077892
  12.9 101.6 %all-gather.6.cloned.1.call-start = ((), (), s32[]{:S(2)}) async-start(), calls=%async_computation.1 | async-start | bytes 9437184 | tf_op jit(solution)/shard_map/all_gather | solution.py:45
  79.2 1.8 %copy-start.4 = (f32[1,2,3072]{2,1,0:T(2,128)S(1)}, f32[1,2,3072]{2,1,0:T(2,128)}, u32[]{:S(2)}) copy-start(f32[1,2,3072]{2,1,0:T(2,128)} %param.6) | copy-start | bytes 73732
  114.5 3.5 %copy-start.5 = (f32[1,1,3072]{2,1,0:T(1,128)S(1)}, f32[1,1,3072]{2,1,0:T(1,128)}, u32[]{:S(2)}) copy-start(f32[1,1,3072]{2,1,0:T(1,128)} %get-tuple-element.20) | copy-start | bytes 36868
  114.5 3.5 %copy-start.8 = (f32[384]{0:T(512)S(1)}, f32[384]{0:T(512)}, u32[]{:S(2)}) copy-start(f32[384]{0:T(512)} %add_rsqrt_fusion.2) | copy-start | bytes 4612
  118.0 2.7 %copy-start = (bf16[2,12,2,64,1024]{4,3,2,1,0:T(8,128)(2,1)}, bf16[2,12,2,64,1024]{4,3,2,1,0:T(8,128)(2,1)S(1)}, u32[]{:S(2)}) copy-start(bf16[2,12,2,64,1024]{4,3,2,1,0:T(8,128)(2,1)S(1)} %copy.45) | copy-start | bytes 18874372
  120.9 2.2 %copy-start.6 = (f32[256]{0:T(256)S(1)}, f32[256]{0:T(256)}, u32[]{:S(2)}) copy-start(f32[256]{0:T(256)} %get-tuple-element.25) | copy-start | bytes 3076
  121.0 2.2 %copy-start.7 = (f32[256]{0:T(256)S(1)}, f32[256]{0:T(256)}, u32[]{:S(2)}) copy-start(f32[256]{0:T(256)} %get-tuple-element.26) | copy-start | bytes 3076
  122.2 4.8 %copy-start.10 = (s32[3]{0:T(128)S(1)}, s32[3]{0:T(128)}, u32[]{:S(2)}) copy-start(s32[3]{0:T(128)} %multiply_add_fusion) | copy-start | bytes 40
  123.4 9.7 %collective-permute-start = (bf16[256,512]{1,0:T(8,128)(2,1)S(1)}, bf16[256,512]{1,0:T(8,128)(2,1)S(1)}, u32[]{:S(2)}, u32[]{:S(2)}) collective-permute-start(bf16[256,512]{1,0:T(8,128)(2,1)S(1)} %get-tuple-element.18), channel_id=1, source_target_pairs={{0,1},{1,2},{2,3},{3,4},{4,5},{5,6},{6,7},{7,8},{8,9},{9,10},{10,1... | collective-permute-start | bytes 786440 | tf_op jit(solution)/shard_map/ppermute | solution.py:27
  125.7 17.6 %collective-permute-start.1 = (bf16[256,512]{1,0:T(8,128)(2,1)S(1)}, bf16[256,512]{1,0:T(8,128)(2,1)S(1)}, u32[]{:S(2)}, u32[]{:S(2)}) collective-permute-start(bf16[256,512]{1,0:T(8,128)(2,1)S(1)} %get-tuple-element.17), channel_id=1, source_target_pairs={{1,0},{2,1},{3,2},{4,3},{5,4},{6,5},{7,6},{8,7},{9,8},{10,9},{11,1... | collective-permute-start | bytes 786440 | tf_op jit(solution)/shard_map/ppermute | solution.py:29
  149.8 1.0 copy-start.2
  150.9 0.9 copy-start.3
Sparse Core Ops, SparseCore 0:
  13.0 64.9 all-gather.3
  80.4 34.0 all-gather.5
where the time goes:
time: 164 us
  waiting for transfers between devices  113 us (69%)
  local copies, waits for them, and re-layouts  15.2 us (9%)
  between operations  13.7 us (8%)
  matrix products  7.35 us (4%)
  blocking collectives  5.36 us (3%)
  other arithmetic  5.25 us (3%)
  starting transfers between devices  3.66 us (2%)
    all_gather x2, waiting for transfers between devices, all_blocks(): parts = lax.all_gather(parts, axes[k], axis=0, tiled=True)  98 us
    ppermute x1, waiting for transfers between devices, with_halo(): lax.ppermute(head, axis, [((i + 1) % count, i) for i in range(ends)])  10.2 us
    all_gather x1, blocking collectives, all_blocks(): parts = lax.all_gather(parts, axes[k], axis=0, tiled=True)  5.36 us
    ppermute x1, waiting for transfers between devices, with_halo(): lax.ppermute(tail, axis, [(i, (i + 1) % count) for i in range(ends)])  4.98 us
    reshape x5, local copies, waits for them, and re-layouts, on_device(): padded[offset * TILE:offset * TILE + rows_here]  4.8 us
    dot_general x1, matrix products, on_device(): lax.dot_general(attended, stashed, (((1,), (1,)), ((), ())), preferred_el...  3.63 us
    transpose x1, local copies, waits for them, and re-layouts, all_blocks(): parts.transpose(*turned, *range(len(sequence), parts.ndim))  3.51 us
  transfers between devices with their start and end apart: 4, of which 4 were waited for; matrix products, arithmetic and copies ran while one was open for 3% of the time, Pallas kernels for 0%

commit v1 on v0

v1 whole, which is shorter than its diff:
```python
import functools
import math

import jax
import jax.numpy as jnp
from jax import lax
from jax.experimental import pallas as pl
from jax.experimental.pallas import tpu as pltpu
from jax.sharding import Mesh
from jax.sharding import PartitionSpec as P

HEAD_DIM = 128
HEADS = 2
TILE = 128
BORDER = 256
WIDTH = HEADS * HEAD_DIM
ROWS = 64
MESH = pl.DeviceIdType.MESH
AXES = ("yl", "z", "c", "x", "yh")
KEY, VALUE, QUERY, OUT = 0, 1, 2, 3
NORM_ROWS = 16


class Counter:
    def __init__(self):
        self.ids = {}

    def __call__(self, *key):
        return self.ids.setdefault(key, len(self.ids))


def head_norm(block, gain):
    parts = []
    for head in range(HEADS):
        part = block[:, head * HEAD_DIM : (head + 1) * HEAD_DIM]
        squares = jnp.mean(part * part, axis=-1, keepdims=True)
        parts.append(part * lax.rsqrt(squares + 1e-06) * gain)
    return jnp.concatenate(parts, axis=1).astype(jnp.bfloat16)


def kernel(
    sizes,
    copies,
    frames,
    modulation,
    w_qkv,
    qk_gain,
    w_out,
    attended,
    out_rows,
    weights,
    raw,
    normed,
    mod,
    gain,
    w_out_here,
    acc,
    padded,
    query,
    top,
    bottom,
    local_sems,
    send_sems,
    recv_sems,
):
    n, nx, nyh = sizes
    half = n // 2
    rows = raw.shape[0]
    tiles = rows // TILE
    yl, z, c = lax.axis_index("yl"), lax.axis_index("z"), lax.axis_index("c")
    x, yh = lax.axis_index("x"), lax.axis_index("yh")
    other = 1 - yl
    frame = x * nyh + yh
    z_next = [{"z": lax.rem(z + 1, n)}, {"z": lax.rem(z + n - 1, n)}]
    y_next = [
        {"yl": other, "yh": lax.rem(yh + yl, nyh)},
        {"yl": other, "yh": lax.rem(yh + nyh - other, nyh)},
    ]
    sibling = {"c": 1 - c}
    after = {"yh": lax.rem(yh + 1, nyh), "x": lax.rem(x + (yh + 1) // nyh, nx)}
    before = {
        "yh": lax.rem(yh + nyh - 1, nyh),
        "x": lax.rem(x + nx - 1 + (yh + nyh - 1) // nyh, nx),
    }

    def far(d, s):
        return lax.rem(z + n + (-s if d == 0 else s), n)

    def local(src, dst, i):
        copy = pltpu.make_async_copy(src, dst, local_sems.at[i])
        copy.start()
        return copy

    own = weights.at[yl, z, c]
    loads = [
        local(w_qkv.at[:, WIDTH : 2 * WIDTH], own.at[KEY], 0),
        local(w_qkv.at[:, 2 * WIDTH :], own.at[VALUE], 1),
        local(w_qkv.at[:, :WIDTH], own.at[QUERY], 2),
        local(w_out, w_out_here, 3),
        local(modulation, mod, 4),
        local(qk_gain, gain, 5),
        local(frames, raw, 6),
    ]

    sent = []

    def remote(src, dst, to, *key):
        i = copies(*key)
        return pltpu.make_async_remote_copy(
            src, dst, send_sems.at[i], recv_sems.at[i], device_id=to, device_id_type=MESH
        )

    def send(ref, to, *key, dst=None):
        copy = remote(ref, ref if dst is None else dst, to, *key)
        copy.start()
        sent.append(copy)

    def arrived(ref, to, *key):
        remote(ref, ref, to, *key).wait_recv()

    barrier = pltpu.get_barrier_semaphore()
    for to in (*z_next, *y_next, sibling, after, before):
        pl.semaphore_signal(barrier, inc=1, device_id=to, device_id_type=MESH)
    pl.semaphore_wait(barrier, 7)

    def kv(row, d, s):
        return weights.at[row, far(d, s), c]

    loads[0].wait()
    loads[1].wait()
    for u in (0, 1):
        for d in (0, 1):
            send(own.at[u], z_next[d], "kv z", u, d, 1)
    for d in (0, 1):
        send(own.at[d], y_next[d], "kv y", d, d, 0)
    send(own.at[0:2], sibling, "kv s", 0, 0, 0)
    loads[2].wait()
    send(own.at[QUERY], y_next[0], "q y")
    send(own.at[QUERY], sibling, "q s own")

    loads[3].wait()
    own[OUT] = w_out_here[...].astype(jnp.float32).T.astype(jnp.bfloat16)

    loads[4].wait()
    loads[5].wait()
    loads[6].wait()

    def norm_step(i, carry):
        at = pl.ds(pl.multiple_of(i * NORM_ROWS, NORM_ROWS), NORM_ROWS)
        full = raw[at, :].astype(jnp.float32)
        centered = full - jnp.mean(full, axis=-1, keepdims=True)
        spread = jnp.mean(centered * centered, axis=-1, keepdims=True)
        scaled = centered * lax.rsqrt(spread + 1e-06)
        normed[at, :] = (scaled * (1.0 + mod[0:1, :]) + mod[1:2, :]).astype(jnp.bfloat16)
        return carry

    lax.fori_loop(0, rows // NORM_ROWS, norm_step, 0)
    send(own.at[OUT], y_next[1], "o y")
    send(own.at[OUT], sibling, "o s own")

    def from_core(row, d, s):
        kind = "kv s" if row is yl else "kv t"
        if s == 0 and row is yl:
            arrived(weights.at[yl, z, 1 - c, 0:2], sibling, kind, 0, 0, 0)
        elif s in (0, half):
            arrived(weights.at[row, far(d, s), 1 - c, d], sibling, kind, d, s)
        else:
            arrived(weights.at[row, far(d, s), 1 - c, 0:2], sibling, kind, d, s)

    def shards(row, s):
        for d in (0, 1):
            if not (s == 0 and row is yl and d == 1):
                from_core(row, d, s)
        return [(row, far(d, s)) for d in ((0,) if s in (0, half) else (0, 1))]

    def accumulate(first, places):
        lhs = jnp.concatenate(
            [
                normed[:, pl.ds(pl.multiple_of((row * n + at) * 2 * ROWS, 2 * ROWS), 2 * ROWS)]
                for row, at in places
            ],
            axis=1,
        )
        for u in (KEY, VALUE):
            rhs = jnp.concatenate(
                [weights[row, at, :, u].reshape(2 * ROWS, WIDTH) for row, at in places], axis=0
            )
            part = jnp.dot(lhs, rhs, preferred_element_type=jnp.float32)
            if first:
                acc[:, u * WIDTH : (u + 1) * WIDTH] = part
            else:
                acc[:, u * WIDTH : (u + 1) * WIDTH] += part

    def across(s):
        for d in (0, 1):
            for u in (0, 1):
                if s in (0, half) and u != d:
                    continue
                arrived(kv(other, d, s).at[u], y_next[1 - d], "kv y", u, d, s)
            ref = kv(other, d, s)
            send(ref.at[d] if s in (0, half) else ref.at[0:2], sibling, "kv t", d, s)

    places = []
    for s in range(1, half + 1):
        for u in (0, 1):
            for d in (0, 1):
                if s == half and u != d:
                    continue
                ref = kv(yl, d, s)
                arrived(ref.at[u], z_next[1 - d], "kv z", u, d, s)
                if s < half - 1 or (s == half - 1 and u == d):
                    send(ref.at[u], z_next[d], "kv z", u, d, s + 1)
                send(ref.at[u], y_next[d], "kv y", u, d, s)
        for d in (0, 1):
            ref = kv(yl, d, s)
            send(ref.at[d] if s == half else ref.at[0:2], sibling, "kv s", d, s)
        if s == half - 1:
            start_ring = True
            arrived(weights.at[other, z, c, QUERY], y_next[1], "q y")
            for d in (0, 1):
                send(weights.at[yl, z, c, QUERY], z_next[d], "q z", 0, d, 1)
            for d in (0, 1):
                send(weights.at[other, z, c, QUERY], z_next[d], "q z", 1, d, 1)
            send(weights.at[other, z, c, QUERY], sibling, "q s other")
        across(s - 1)
        places += shards(yl, s - 1)
        if s >= 2:
            places += shards(other, s - 2)
            accumulate(s == 2, places)
            places = []
    across(half)
    places = shards(yl, half) + shards(other, half - 1) + shards(other, half)
    accumulate(False, places)

    padded[BORDER : BORDER + rows, :WIDTH] = head_norm(acc[:, :WIDTH], gain[1:2, :])
    padded[BORDER : BORDER + rows, WIDTH:] = acc[:, WIDTH:].astype(jnp.bfloat16)
    send(
        padded.at[BORDER : 2 * BORDER],
        before,
        "head",
        dst=padded.at[BORDER + rows : 2 * BORDER + rows],
    )
    send(padded.at[rows : rows + BORDER], after, "tail", dst=padded.at[0:BORDER])

    def ring_step(name, b, s):
        for u in (0, 1):
            row = yl if u == 0 else other
            for d in (0, 1):
                if s == half and u != d:
                    continue
                ref = weights.at[row, far(d, s), c, b]
                arrived(ref, z_next[1 - d], name + " z", u, d, s)
                if s < half - 1 or (s == half - 1 and u == d):
                    send(ref, z_next[d], name + " z", u, d, s + 1)
                send(ref, sibling, name + " s", u, d, s)

    def ring_end(name, b):
        arrived(weights.at[yl, z, 1 - c, b], sibling, name + " s own")
        arrived(weights.at[other, z, 1 - c, b], sibling, name + " s other")
        for s in range(1, half + 1):
            for u in (0, 1):
                row = yl if u == 0 else other
                for d in (0, 1):
                    if s == half and u != d:
                        continue
                    arrived(weights.at[row, far(d, s), 1 - c, b], sibling, name + " s", u, d, s)

    def project_queries():
        depth = 8 * ROWS
        steps = n // 4

        def step(k, carry):
            lhs = normed[:, pl.ds(pl.multiple_of(k * depth, depth), depth)]
            rhs = weights[k // steps, pl.ds(lax.rem(k, steps) * 4, 4), :, QUERY]
            part = jnp.dot(lhs, rhs.reshape(depth, WIDTH), preferred_element_type=jnp.float32)
            return carry + part

        total = lax.fori_loop(0, 2 * steps, step, jnp.zeros((rows, WIDTH), jnp.float32))
        query[...] = head_norm(total, gain[0:1, :])

    scale = 1.0 / math.sqrt(HEAD_DIM)

    def part_of(tile, head, start, count, weight=None):
        cols = slice(head * HEAD_DIM, (head + 1) * HEAD_DIM)
        q = query[tile * TILE : (tile + 1) * TILE, cols]
        k = padded[start : start + count, cols]
        v = padded[start : start + count, WIDTH + head * HEAD_DIM : WIDTH + (head + 1) * HEAD_DIM]
        score = lax.dot_general(
            q, k, (((1,), (1,)), ((), ())), preferred_element_type=jnp.float32
        )
        raised = jnp.exp(score * scale)
        if weight is not None:
            raised = raised * weight
        low = jnp.sum(raised, axis=-1, keepdims=True)
        high = jnp.dot(raised.astype(jnp.bfloat16), v, preferred_element_type=jnp.float32)
        return high, jnp.broadcast_to(low, (TILE, HEAD_DIM))

    def near_part(tile):
        for head in range(HEADS):
            high, low = part_of(tile, head, BORDER, rows)
            top[tile, head] = high
            bottom[tile, head] = low

    for s in range(1, half + 1):
        ring_step("q", QUERY, s)
        if s == half - 1:
            arrived(weights.at[other, z, c, OUT], y_next[0], "o y")
            for d in (0, 1):
                send(weights.at[yl, z, c, OUT], z_next[d], "o z", 0, d, 1)
            for d in (0, 1):
                send(weights.at[other, z, c, OUT], z_next[d], "o z", 1, d, 1)
            send(weights.at[other, z, c, OUT], sibling, "o s other")
    for s in range(1, half + 1):
        ring_step("o", OUT, s)
        if s == 1:
            ring_end("q", QUERY)
            project_queries()
        if s == 2:
            near_part(0)
        if s == min(3, half):
            near_part(1)
        if s == min(4, half):
            near_part(2)
    ring_end("o", OUT)
    stored = local(weights.at[:, :, :, OUT], out_rows, 0)

    arrived(padded.at[0:BORDER], before, "tail")
    arrived(padded.at[BORDER + rows : 2 * BORDER + rows], after, "head")
    has_before = jnp.where(frame > 0, 1.0, 0.0)
    has_after = jnp.where(frame < nx * nyh - 1, 1.0, 0.0)
    for tile in range(tiles):
        done = []
        for head in range(HEADS):
            high, low = top[tile, head], bottom[tile, head]
            first, last = tile * TILE, (tile + 5) * TILE
            if first < BORDER:
                more, less = part_of(tile, head, first, BORDER - first, has_before)
                high, low = high + more, low + less
            if last > BORDER + rows:
                more, less = part_of(tile, head, BORDER + rows, last - BORDER - rows, has_after)
                high, low = high + more, low + less
            done.append((high / low).astype(jnp.bfloat16))
        attended[tile * TILE : (tile + 1) * TILE, :] = jnp.concatenate(done, axis=1)
    stored.wait()
    for copy in sent:
        copy.wait_send()


def on_device(sizes, frames, modulation, w_qkv, qk_gain, w_out):
    n = sizes[0]
    rows, features = frames.shape[1:]
    copies = Counter()
    anywhere = pl.BlockSpec(memory_space=pl.ANY)
    attended, out_rows = pl.pallas_call(
        functools.partial(kernel, sizes, copies),
        out_shape=(
            jax.ShapeDtypeStruct((rows, WIDTH), jnp.bfloat16),
            jax.ShapeDtypeStruct((2, n, 2, ROWS, WIDTH), jnp.bfloat16),
        ),
        in_specs=[anywhere] * 5,
        out_specs=(pl.BlockSpec(memory_space=pltpu.VMEM), anywhere),
        scratch_shapes=[
            pltpu.VMEM((2, n, 2, 4, ROWS, WIDTH), jnp.bfloat16),
            pltpu.VMEM((rows, features), jnp.bfloat16),
            pltpu.VMEM((rows, features), jnp.bfloat16),
            pltpu.VMEM((2, features), jnp.float32),
            pltpu.VMEM((2, HEAD_DIM), jnp.float32),
            pltpu.VMEM((WIDTH, ROWS), jnp.bfloat16),
            pltpu.VMEM((rows, 2 * WIDTH), jnp.float32),
            pltpu.VMEM((rows + 2 * BORDER, 2 * WIDTH), jnp.bfloat16),
            pltpu.VMEM((rows, WIDTH), jnp.bfloat16),
            pltpu.VMEM((rows // TILE, HEADS, TILE, HEAD_DIM), jnp.float32),
            pltpu.VMEM((rows // TILE, HEADS, TILE, HEAD_DIM), jnp.float32),
            pltpu.SemaphoreType.DMA((7,)),
            pltpu.SemaphoreType.DMA((220,)),
            pltpu.SemaphoreType.DMA((220,)),
        ],
        compiler_params=pltpu.CompilerParams(collective_id=0, has_side_effects=True),
    )(frames[0], modulation[0], w_qkv, qk_gain, w_out)
    mixed = lax.dot_general(
        attended,
        out_rows.reshape(features, WIDTH),
        (((1,), (1,)), ((), ())),
        preferred_element_type=jnp.float32,
    ).astype(jnp.bfloat16)
    return mixed[None]


def solution(mesh, n=12, nx=4, nyh=4):
    finer = Mesh(mesh.devices.reshape(2, n, 2, nx, nyh), AXES)
    fsdp, frame = ("yl", "z", "c"), ("x", "yh")
    placed = (P(fsdp, frame, None), P(fsdp, None, None), P(fsdp, None), P(), P(None, fsdp))
    return jax.shard_map(
        functools.partial(on_device, (n, nx, nyh)),
        mesh=finer,
        in_specs=placed,
        out_specs=P(fsdp, frame, None),
        check_vma=False,
    )
```

time: 164 us -> 92.1 us (0.56)
  waiting for transfers between devices: 113 us -> 0 us
  Pallas kernels: 0 us -> 86.6 us
  local copies, waits for them, and re-layouts: 15.2 us -> 1.49 us
  between operations: 13.7 us -> 0.01 us
  blocking collectives: 5.36 us -> 0 us
  other arithmetic: 5.25 us -> 0 us
  starting transfers between devices: 3.66 us -> 0 us
  matrix products: 7.35 us -> 3.75 us
    all_gather x2 -> x0, waiting for transfers between devices: 98 us -> none  [all_blocks(): parts = lax.all_gather(parts, axes[k], axis=0, tiled=True)]
    pallas_call x0 -> x1, Pallas kernels: none -> 86.6 us  [on_device(): pl.pallas_call(functools.partial(kernel, sizes, copies), out_shape=(jax.S...]
    ppermute x2 -> x0, waiting for transfers between devices: 15.2 us -> none  [the longest x1 10.2 us: with_halo(): lax.ppermute(head, axis, [((i + 1) % count, i) for i in range(ends)])]
    reshape x6 -> x0, local copies, waits for them, and re-layouts: 5.53 us -> none  [the longest x5 4.8 us: on_device(): padded[offset * TILE:offset * TILE + rows_here]]
    all_gather x1 -> x0, blocking collectives: 5.36 us -> none  [all_blocks(): parts = lax.all_gather(parts, axes[k], axis=0, tiled=True)]
    ppermute x2 -> x0, starting transfers between devices: 3.61 us -> none  [the longest x1 2.32 us: with_halo(): lax.ppermute(tail, axis, [(i, (i + 1) % count) for i in range(ends)])]
    dot_general x4 -> x1, matrix products: 7.35 us -> 3.75 us  [on_device(): lax.dot_general(attended, out_rows.reshape(features, WIDTH), (((1,), (1,)...]
    transpose x1 -> x0, local copies, waits for them, and re-layouts: 3.51 us -> none  [all_blocks(): parts.transpose(*turned, *range(len(sequence), parts.ndim))]
  transfers between devices with their start and end apart: 4 -> 0, of which waited for: 4 -> 0; matrix products, arithmetic and copies ran while one was open for 3% -> 0% of each run, Pallas kernels for 0% -> 0%
where the time goes in v1:
time: 92.1 us; the launch traced here: 91.9 us
  Pallas kernels  86.6 us (94%)
  matrix products  3.75 us (4%)
  local copies, waits for them, and re-layouts  1.49 us (2%)
    pallas_call x1, Pallas kernels, on_device(): pl.pallas_call(functools.partial(kernel, sizes, copies), out_shape=(jax.S...  86.6 us
    dot_general x1, matrix products, on_device(): lax.dot_general(attended, out_rows.reshape(features, WIDTH), (((1,), (1,)...  3.75 us

profile of v1, /device:TPU:1, one launch (start us, length us, event | category | flops | bytes accessed | tf_op | source)
XLA Modules:
  0.0 91.9 jit_solution(18282152368804881083)
XLA Ops:
  0.0 1.5 %copy.6.w_out = bf16[256,64]{1,0:T(8,128)(2,1)} copy(bf16[256,64]{0,1:T(8,128)(2,1)} %param.9) | data formatting | bytes 65536 | tf_op args[4]
  1.5 86.6 %shard_map.55 = (bf16[384,256]{1,0:T(8,128)(2,1)}, bf16[2,12,2,64,256]{4,3,2,1,0:T(8,128)(2,1)}) custom-call(bf16[384,3072]{1,0:T(8,128)(2,1)} %bitcast.7, f32[2,3072]{1,0:T(2,128)} %bitcast.9, bf16[64,768]{1,0:T(8,128)(2,1)} %w_qkv.1, f32[2,128]{1,0:T(2,128)} %qk_gain.1, bf16[256,64]{1,0:T(8,128)(2,1)} %copy.6.w_out), custom_call_target="tpu_custom_call" | custom-call | tf_op jit(solution)/shard_map/pallas_call | solution.py:354
  88.1 3.7 %fusion = bf16[1,384,3072]{2,1,0:T(8,128)(2,1)} fusion(bf16[384,256]{1,0:T(8,128)(2,1)} %get-tuple-element.7, bf16[3072,256]{1,0:T(8,128)(2,1)} %bitcast.8), kind=kOutput, calls=%fused_computation.1 | convolution fusion | flops 605159424 | bytes 4128768 | tf_op jit(solution)/shard_map/dot_general | solution.py:380

commit v2 on v1

v2 whole, which is shorter than its diff:
```python
import functools
import math

import jax
import jax.numpy as jnp
from jax import lax
from jax.experimental import pallas as pl
from jax.experimental.pallas import tpu as pltpu
from jax.sharding import Mesh
from jax.sharding import PartitionSpec as P

HEAD_DIM = 128
HEADS = 2
TILE = 128
BORDER = 256
WIDTH = HEADS * HEAD_DIM
ROWS = 64
MESH = pl.DeviceIdType.MESH
AXES = ("yl", "z", "c", "x", "yh")
KEY, VALUE = 0, 1
QUERY, OUT = 0, 1
PARTS = 4
PIECE = ROWS // PARTS
NORM_ROWS = 16


class Counter:
    def __init__(self):
        self.ids = {}

    def __call__(self, *key):
        return self.ids.setdefault(key, len(self.ids))


def head_norm(block, gain):
    parts = []
    for head in range(HEADS):
        part = block[:, head * HEAD_DIM : (head + 1) * HEAD_DIM]
        squares = jnp.mean(part * part, axis=-1, keepdims=True)
        parts.append(part * lax.rsqrt(squares + 1e-06) * gain)
    return jnp.concatenate(parts, axis=1).astype(jnp.bfloat16)


def stage_slots(half):
    bounds = [0, 5] if half > 2 else [0, 4]
    while bounds[-1] < 2 * half:
        bounds.append(min(bounds[-1] + 4, 2 * half))
    return list(zip(bounds[:-1], bounds[1:]))


def kernel(
    sizes,
    copies,
    frames,
    modulation,
    w_qkv,
    qk_gain,
    w_out_t,
    mixed,
    kv_weights,
    qo_weights,
    raw,
    normed,
    mod,
    gain,
    acc,
    padded,
    query,
    top,
    bottom,
    attended,
    result,
    local_sems,
    send_sems,
    recv_sems,
    out_sems,
):
    n, nx, nyh = sizes
    half = n // 2
    stages = half // 2
    slots = stage_slots(half)
    rows = raw.shape[0]
    tiles = rows // TILE
    yl, z, c = lax.axis_index("yl"), lax.axis_index("z"), lax.axis_index("c")
    x, yh = lax.axis_index("x"), lax.axis_index("yh")
    other = 1 - yl
    frame = x * nyh + yh

    def z_by(d, t):
        return {"z": lax.rem(z + (t if d == 0 else n - t), n)}

    y_next = [
        {"yl": other, "yh": lax.rem(yh + yl, nyh)},
        {"yl": other, "yh": lax.rem(yh + nyh - other, nyh)},
    ]
    x_at = [lax.rem(x + 1, nx), lax.rem(x + nx - 1, nx)]
    x_next = [{"x": x_at[0]}, {"x": x_at[1]}]
    x_far = lax.rem(x + 2, nx)
    sibling = {"c": 1 - c}
    after = {"yh": lax.rem(yh + 1, nyh), "x": lax.rem(x + (yh + 1) // nyh, nx)}
    before = {
        "yh": lax.rem(yh + nyh - 1, nyh),
        "x": lax.rem(x + nx - 1 + (yh + nyh - 1) // nyh, nx),
    }

    def slot(d, s):
        if s == 0:
            return 0
        base = 1 + 4 * ((s - 1) // 2)
        if s >= half - 1:
            return base + (d if s < half else 2)
        return base + 2 * d + (s - 1) % 2

    offset = {0: 0}
    for d in (0, 1):
        for s in range(1, half + 1):
            offset[slot(d, s)] = -s if d == 0 else s

    def column(row, at):
        start = ((yl if row == 0 else other) * n + lax.rem(z + n + offset[at], n)) * 2 * ROWS
        return pl.ds(pl.multiple_of(start, 2 * ROWS), 2 * ROWS)

    def local(src, dst, i):
        copy = pltpu.make_async_copy(src, dst, local_sems.at[i])
        copy.start()
        return copy

    piece = pl.ds(pl.multiple_of(x * PIECE, PIECE), PIECE)
    loads = [
        local(w_qkv.at[:, WIDTH : 2 * WIDTH], kv_weights.at[c, 0, 0, KEY], 0),
        local(w_qkv.at[:, 2 * WIDTH :], kv_weights.at[c, 0, 0, VALUE], 1),
        local(w_qkv.at[piece, :WIDTH], qo_weights.at[x, c, 0, 0, QUERY], 2),
        local(w_out_t.at[piece, :], qo_weights.at[x, c, 0, 0, OUT], 3),
        local(modulation, mod, 4),
        local(qk_gain, gain, 5),
        local(frames, raw, 6),
    ]

    sent = []

    def remote(src, dst, to, *key):
        i = copies(*key)
        return pltpu.make_async_remote_copy(
            src, dst, send_sems.at[i], recv_sems.at[i], device_id=to, device_id_type=MESH
        )

    def send(ref, to, *key, dst=None):
        copy = remote(ref, ref if dst is None else dst, to, *key)
        copy.start()
        sent.append(copy)

    def arrived(ref, to, *key):
        remote(ref, ref, to, *key).wait_recv()

    barrier = pltpu.get_barrier_semaphore()
    partners = [z_by(d, t) for d in (0, 1) for t in (1, 2)]
    partners += [*y_next, *x_next, sibling, after, before]
    for to in partners:
        pl.semaphore_signal(barrier, inc=1, device_id=to, device_id_type=MESH)
    pl.semaphore_wait(barrier, len(partners))

    def kv_at(u, d, s):
        return kv_weights.at[c, 0, slot(d, s), u]

    def kv_pass(u, d, s, t):
        if s + t < half or (s + t == half and u == d):
            send(kv_at(u, d, s), z_by(d, t), "kv z", u, d, s + t, dst=kv_at(u, d, s + t))

    def qo_at(d, s):
        if s == half:
            return qo_weights.at[x, c, d, slot(d, s)]
        return qo_weights.at[x, c, :, slot(d, s)]

    def qo_pass(d, s, t):
        if s + t <= half:
            row = d if s + t == half else slice(None)
            src = qo_weights.at[x, c, row, slot(d, s)]
            send(src, z_by(d, t), "qo z", d, s + t, dst=qo_at(d, s + t))

    def normalize(first, last):
        def norm_step(i, carry):
            at = pl.ds(pl.multiple_of(i * NORM_ROWS, NORM_ROWS), NORM_ROWS)
            full = raw[at, :].astype(jnp.float32)
            centered = full - jnp.mean(full, axis=-1, keepdims=True)
            spread = jnp.mean(centered * centered, axis=-1, keepdims=True)
            scaled = centered * lax.rsqrt(spread + 1e-06)
            normed[at, :] = (scaled * (1.0 + mod[0:1, :]) + mod[1:2, :]).astype(jnp.bfloat16)
            return carry

        lax.fori_loop(first // NORM_ROWS, last // NORM_ROWS, norm_step, 0)

    def accumulate(first, places):
        lhs = jnp.concatenate([normed[:, column(row, at)] for row, at in places], axis=1)
        for u in (KEY, VALUE):
            rhs = jnp.concatenate(
                [kv_weights[:, row, at, u].reshape(2 * ROWS, WIDTH) for row, at in places], axis=0
            )
            part = jnp.dot(lhs, rhs, preferred_element_type=jnp.float32)
            if first:
                acc[:, u * WIDTH : (u + 1) * WIDTH] = part
            else:
                acc[:, u * WIDTH : (u + 1) * WIDTH] += part

    def places_of(row, g):
        a, b = slots[g]
        arrived(kv_weights.at[1 - c, row, a:b], sibling, "kv s", row, g)
        return [(row, at) for at in range(a, b)]

    def stage_parts(g, d):
        odd = 2 * g + 1
        at = slot(d, odd)
        if odd + 1 < half:
            return [(slice(at, at + 2), slice(None))]
        return [(slice(at, at + 1), slice(None)), (slice(2 * half - 1, 2 * half), slice(d, d + 1))]

    def across(g):
        for d in (0, 1):
            for i, (at, u) in enumerate(stage_parts(g, d)):
                ref, dst = kv_weights.at[c, 0, at, u], kv_weights.at[c, 1, at, u]
                send(ref, y_next[d], "kv y", g, d, i, dst=dst)

    def from_across(g):
        for d in (0, 1):
            if g == 0:
                arrived(kv_weights.at[c, 1, 0, d], y_next[1 - d], "kv y own", d)
            for i, (at, u) in enumerate(stage_parts(g, d)):
                arrived(kv_weights.at[c, 1, at, u], y_next[1 - d], "kv y", g, d, i)
        a, b = slots[g]
        send(kv_weights.at[c, 1, a:b], sibling, "kv s", 1, g)

    def qo_across_x(g):
        a, b = slots[g]
        for d in (0, 1):
            send(qo_weights.at[x, c, :, a:b], x_next[d], "qo x", g, d)

    def qo_relay_x(g):
        a, b = slots[g]
        for d in (0, 1):
            arrived(qo_weights.at[x_at[1 - d], c, :, a:b], x_next[1 - d], "qo x", g, d)
            send(qo_weights.at[x_at[1 - d], c, d, a:b], x_next[d], "qo r", g, d)

    def qo_to_core(g):
        a, b = slots[g]
        for d in (0, 1):
            arrived(qo_weights.at[x_far, c, d, a:b], x_next[1 - d], "qo r", g, d)
        send(qo_weights.at[:, c, :, a:b], sibling, "qo s", g)

    loads[0].wait()
    loads[1].wait()
    for t in (2, 1):
        for u in (KEY, VALUE):
            for d in (0, 1):
                kv_pass(u, d, 0, t)
    for d in (0, 1):
        ref, dst = kv_weights.at[c, 0, 0, d], kv_weights.at[c, 1, 0, d]
        send(ref, y_next[d], "kv y own", d, dst=dst)
    loads[2].wait()
    loads[3].wait()
    send(qo_weights.at[x, c, 0, 0], y_next[0], "qo y", dst=qo_weights.at[x, c, 1, 0])
    loads[4].wait()
    loads[5].wait()
    loads[6].wait()
    normalize(0, BORDER)
    arrived(qo_weights.at[x, c, 1, 0], y_next[1], "qo y")
    for t in (2, 1):
        for d in (0, 1):
            qo_pass(d, 0, t)

    for g in range(stages):
        even = 2 * g + 2
        for u in (KEY, VALUE):
            for d in (0, 1):
                if even == half and u != d:
                    continue
                arrived(kv_at(u, d, even), z_by(1 - d, 2), "kv z", u, d, even)
                kv_pass(u, d, even, 2)
        for u in (KEY, VALUE):
            for d in (0, 1):
                kv_pass(u, d, even, 1)
        for u in (KEY, VALUE):
            for d in (0, 1):
                arrived(kv_at(u, d, even - 1), z_by(1 - d, 1), "kv z", u, d, even - 1)
        across(g)
        a, b = slots[g]
        send(kv_weights.at[c, 0, a:b], sibling, "kv s", 0, g)
        for d in (0, 1):
            arrived(qo_at(d, even), z_by(1 - d, 2), "qo z", d, even)
            for t in (2, 1):
                qo_pass(d, even, t)
        for d in (0, 1):
            arrived(qo_at(d, even - 1), z_by(1 - d, 1), "qo z", d, even - 1)
        qo_across_x(g)
        if g == 0:
            normalize(BORDER, rows)
        else:
            from_across(g - 1)
            qo_relay_x(g - 1)
            accumulate(g == 1, places_of(0, g - 1) + (places_of(1, g - 2) if g > 1 else []))
    last = stages - 1
    places = places_of(0, last) + (places_of(1, last - 1) if last > 0 else [])
    accumulate(last == 0, places)
    from_across(last)
    accumulate(False, places_of(1, last))

    padded[BORDER : BORDER + rows, :WIDTH] = head_norm(acc[:, :WIDTH], gain[1:2, :])
    padded[BORDER : BORDER + rows, WIDTH:] = acc[:, WIDTH:].astype(jnp.bfloat16)
    send(
        padded.at[BORDER : 2 * BORDER],
        before,
        "head",
        dst=padded.at[BORDER + rows : 2 * BORDER + rows],
    )
    send(padded.at[rows : rows + BORDER], after, "tail", dst=padded.at[0:BORDER])

    qo_relay_x(last)
    for g in range(stages):
        qo_to_core(g)
    for g in range(stages):
        a, b = slots[g]
        arrived(qo_weights.at[:, 1 - c, :, a:b], sibling, "qo s", g)

    def whole(row, at, which):
        return [qo_weights[q, core, row, at, which] for core in (0, 1) for q in range(PARTS)]

    everything = [(row, at) for row in (0, 1) for at in range(n)]
    total = jnp.zeros((rows, WIDTH), jnp.float32)
    for i in range(0, len(everything), 4):
        group = everything[i : i + 4]
        lhs = jnp.concatenate([normed[:, column(row, at)] for row, at in group], axis=1)
        rhs = jnp.concatenate([p for row, at in group for p in whole(row, at, QUERY)], axis=0)
        total = total + jnp.dot(lhs, rhs, preferred_element_type=jnp.float32)
    query[...] = head_norm(total, gain[0:1, :])

    scale = 1.0 / math.sqrt(HEAD_DIM)

    def part_of(tile, head, start, count, weight=None):
        cols = slice(head * HEAD_DIM, (head + 1) * HEAD_DIM)
        q = query[tile * TILE : (tile + 1) * TILE, cols]
        k = padded[start : start + count, cols]
        v = padded[start : start + count, WIDTH + head * HEAD_DIM : WIDTH + (head + 1) * HEAD_DIM]
        score = lax.dot_general(
            q, k, (((1,), (1,)), ((), ())), preferred_element_type=jnp.float32
        )
        raised = jnp.exp(score * scale)
        if weight is not None:
            raised = raised * weight
        low = jnp.sum(raised, axis=-1, keepdims=True)
        high = jnp.dot(raised.astype(jnp.bfloat16), v, preferred_element_type=jnp.float32)
        return high, jnp.broadcast_to(low, (TILE, HEAD_DIM))

    for tile in range(tiles):
        for head in range(HEADS):
            high, low = part_of(tile, head, BORDER, rows)
            top[tile, head] = high
            bottom[tile, head] = low

    arrived(padded.at[0:BORDER], before, "tail")
    arrived(padded.at[BORDER + rows : 2 * BORDER + rows], after, "head")
    has_before = jnp.where(frame > 0, 1.0, 0.0)
    has_after = jnp.where(frame < nx * nyh - 1, 1.0, 0.0)
    for tile in range(tiles):
        done = []
        for head in range(HEADS):
            high, low = top[tile, head], bottom[tile, head]
            first, end = tile * TILE, (tile + 5) * TILE
            if first < BORDER:
                more, less = part_of(tile, head, first, BORDER - first, has_before)
                high, low = high + more, low + less
            if end > BORDER + rows:
                more, less = part_of(tile, head, BORDER + rows, end - BORDER - rows, has_after)
                high, low = high + more, low + less
            done.append((high / low).astype(jnp.bfloat16))
        attended[tile * TILE : (tile + 1) * TILE, :] = jnp.concatenate(done, axis=1)

    stored = []
    for i in range(0, len(everything), 2):
        pair = everything[i : i + 2]
        rhs = jnp.concatenate([p for row, at in pair for p in whole(row, at, OUT)], axis=0)
        part = lax.dot_general(
            attended[...], rhs, (((1,), (1,)), ((), ())), preferred_element_type=jnp.float32
        ).astype(jnp.bfloat16)
        for j, (row, at) in enumerate(pair):
            result[i + j] = part[:, j * 2 * ROWS : (j + 1) * 2 * ROWS]
            copy = pltpu.make_async_copy(
                result.at[i + j], mixed.at[:, column(row, at)], out_sems.at[i + j]
            )
            copy.start()
            stored.append(copy)
    for copy in stored:
        copy.wait()
    for copy in sent:
        copy.wait_send()


def on_device(sizes, frames, modulation, w_qkv, qk_gain, w_out):
    n = sizes[0]
    rows, features = frames.shape[1:]
    anywhere = pl.BlockSpec(memory_space=pl.ANY)
    mixed = pl.pallas_call(
        functools.partial(kernel, sizes, Counter()),
        out_shape=jax.ShapeDtypeStruct((rows, features), jnp.bfloat16),
        in_specs=[anywhere] * 5,
        out_specs=anywhere,
        scratch_shapes=[
            pltpu.VMEM((2, 2, n, 2, ROWS, WIDTH), jnp.bfloat16),
            pltpu.VMEM((PARTS, 2, 2, n, 2, PIECE, WIDTH), jnp.bfloat16),
            pltpu.VMEM((rows, features), jnp.bfloat16),
            pltpu.VMEM((rows, features), jnp.bfloat16),
            pltpu.VMEM((2, features), jnp.float32),
            pltpu.VMEM((2, HEAD_DIM), jnp.float32),
            pltpu.VMEM((rows, 2 * WIDTH), jnp.float32),
            pltpu.VMEM((rows + 2 * BORDER, 2 * WIDTH), jnp.bfloat16),
            pltpu.VMEM((rows, WIDTH), jnp.bfloat16),
            pltpu.VMEM((rows // TILE, HEADS, TILE, HEAD_DIM), jnp.float32),
            pltpu.VMEM((rows // TILE, HEADS, TILE, HEAD_DIM), jnp.float32),
            pltpu.VMEM((rows, WIDTH), jnp.bfloat16),
            pltpu.VMEM((2 * n, rows, 2 * ROWS), jnp.bfloat16),
            pltpu.SemaphoreType.DMA((7,)),
            pltpu.SemaphoreType.DMA((96,)),
            pltpu.SemaphoreType.DMA((96,)),
            pltpu.SemaphoreType.DMA((2 * n,)),
        ],
        compiler_params=pltpu.CompilerParams(collective_id=0, has_side_effects=True),
    )(frames[0], modulation[0], w_qkv, qk_gain, jnp.transpose(w_out))
    return mixed[None]


def solution(mesh, n=12, nx=4, nyh=4):
    finer = Mesh(mesh.devices.reshape(2, n, 2, nx, nyh), AXES)
    fsdp, frame = ("yl", "z", "c"), ("x", "yh")
    placed = (P(fsdp, frame, None), P(fsdp, None, None), P(fsdp, None), P(), P(None, fsdp))
    return jax.shard_map(
        functools.partial(on_device, (n, nx, nyh)),
        mesh=finer,
        in_specs=placed,
        out_specs=P(fsdp, frame, None),
        check_vma=False,
    )
```

time: 92.1 us -> 64 us (0.69)
  Pallas kernels: 86.6 us -> 59.9 us
  matrix products: 3.75 us -> 0 us
  local copies, waits for them, and re-layouts: 1.49 us -> 3.22 us
    pallas_call x1, Pallas kernels: 86.6 us -> 59.9 us  [on_device(): pl.pallas_call(functools.partial(kernel, sizes, Counter()), out_shape=jax...]
    dot_general x1 -> x0, matrix products: 3.75 us -> none  [on_device(): lax.dot_general(attended, out_rows.reshape(features, WIDTH), (((1,), (1,)...]
    unnamed x1, local copies, waits for them, and re-layouts: 1.49 us -> 3.22 us
where the time goes in v2:
time: 64 us; the launch traced here: 63.1 us
  Pallas kernels  59.9 us (94%)
  local copies, waits for them, and re-layouts  3.22 us (5%)
    pallas_call x1, Pallas kernels, on_device(): pl.pallas_call(functools.partial(kernel, sizes, Counter()), out_shape=jax...  59.9 us
    unnamed x1, local copies, waits for them, and re-layouts  3.22 us

profile of v2, /device:TPU:1, one launch (start us, length us, event | category | flops | bytes accessed | tf_op | source)
XLA Modules:
  0.0 63.1 jit_solution(6736791439323250855)
XLA Ops:
  0.0 59.9 %shard_map.55 = bf16[384,3072]{1,0:T(8,128)(2,1)} custom-call(bf16[384,3072]{1,0:T(8,128)(2,1)} %bitcast.5, f32[2,3072]{1,0:T(2,128)} %bitcast.7, bf16[64,768]{1,0:T(8,128)(2,1)} %w_qkv.1, f32[2,128]{1,0:T(2,128)} %qk_gain.1, bf16[64,256]{1,0:T(8,128)(2,1)} %bitcast.6), custom_call_target="tpu_custom_call" | custom-call | tf_op jit(solution)/shard_map/pallas_call | solution.py:399
  59.9 3.2 %copy.7 = bf16[1,384,3072]{2,1,0:T(8,128)(2,1)} copy(bf16[1,384,3072]{2,1,0:T(8,128)(2,1)} %bitcast.4) | data formatting | bytes 4718592

commit v3 on v2

v3 whole, which is shorter than its diff:
```python
import functools
import math

import jax
import jax.numpy as jnp
from jax import lax
from jax.experimental import pallas as pl
from jax.experimental.pallas import tpu as pltpu
from jax.sharding import Mesh
from jax.sharding import PartitionSpec as P

HEAD_DIM = 128
HEADS = 2
TILE = 128
BORDER = 256
WIDTH = HEADS * HEAD_DIM
ROWS = 64
MESH = pl.DeviceIdType.MESH
AXES = ("yl", "z", "c", "x", "yh")
KEY, VALUE = 0, 1
QUERY, OUT = 0, 1
PARTS = 4
PIECE = ROWS // PARTS
NORM_ROWS = 16


class Counter:
    def __init__(self):
        self.ids = {}

    def __call__(self, *key):
        return self.ids.setdefault(key, len(self.ids))


def head_norm(block, gain):
    parts = []
    for head in range(HEADS):
        part = block[:, head * HEAD_DIM : (head + 1) * HEAD_DIM]
        squares = jnp.mean(part * part, axis=-1, keepdims=True)
        parts.append(part * lax.rsqrt(squares + 1e-06) * gain)
    return jnp.concatenate(parts, axis=1).astype(jnp.bfloat16)


def stage_slots(half):
    bounds = [0, 5] if half > 2 else [0, 4]
    while bounds[-1] < 2 * half:
        bounds.append(min(bounds[-1] + 4, 2 * half))
    return list(zip(bounds[:-1], bounds[1:]))


def kernel(
    sizes,
    copies,
    frames,
    modulation,
    w_qkv,
    qk_gain,
    w_out_t,
    attended,
    out_rows,
    kv_weights,
    qo_weights,
    raw,
    normed,
    mod,
    gain,
    acc,
    keys,
    values,
    query,
    top,
    bottom,
    shares,
    local_sems,
    send_sems,
    recv_sems,
):
    n, nx, nyh = sizes
    half = n // 2
    stages = half // 2
    slots = stage_slots(half)
    rows = raw.shape[0]
    tiles = rows // TILE
    yl, z, c = lax.axis_index("yl"), lax.axis_index("z"), lax.axis_index("c")
    x, yh = lax.axis_index("x"), lax.axis_index("yh")
    other = 1 - yl
    frame = x * nyh + yh

    def z_by(d, t):
        return {"z": lax.rem(z + (t if d == 0 else n - t), n)}

    y_next = [
        {"yl": other, "yh": lax.rem(yh + yl, nyh)},
        {"yl": other, "yh": lax.rem(yh + nyh - other, nyh)},
    ]
    x_at = [lax.rem(x + 1, nx), lax.rem(x + nx - 1, nx)]
    x_next = [{"x": x_at[0]}, {"x": x_at[1]}]
    x_far = lax.rem(x + 2, nx)
    sibling = {"c": 1 - c}
    after = {"yh": lax.rem(yh + 1, nyh), "x": lax.rem(x + (yh + 1) // nyh, nx)}
    before = {
        "yh": lax.rem(yh + nyh - 1, nyh),
        "x": lax.rem(x + nx - 1 + (yh + nyh - 1) // nyh, nx),
    }

    def slot(d, s):
        if s == 0:
            return 0
        base = 1 + 4 * ((s - 1) // 2)
        if s >= half - 1:
            return base + (d if s < half else 2)
        return base + 2 * d + (s - 1) % 2

    offset = {0: 0}
    for d in (0, 1):
        for s in range(1, half + 1):
            offset[slot(d, s)] = -s if d == 0 else s

    def column(row, at):
        start = ((yl if row == 0 else other) * n + lax.rem(z + n + offset[at], n)) * 2 * ROWS
        return pl.ds(pl.multiple_of(start, 2 * ROWS), 2 * ROWS)

    def local(src, dst, i):
        copy = pltpu.make_async_copy(src, dst, local_sems.at[i])
        copy.start()
        return copy

    piece = pl.ds(pl.multiple_of(x * PIECE, PIECE), PIECE)
    loads = [
        local(w_qkv.at[:, WIDTH : 2 * WIDTH], kv_weights.at[c, 0, KEY, 0], 0),
        local(w_qkv.at[:, 2 * WIDTH :], kv_weights.at[c, 0, VALUE, 0], 1),
        local(w_qkv.at[piece, :WIDTH], qo_weights.at[x, c, 0, 0, QUERY], 2),
        local(w_out_t.at[piece, :], qo_weights.at[x, c, 0, 0, OUT], 3),
        local(modulation, mod, 4),
        local(qk_gain, gain, 5),
        local(frames, raw, 6),
    ]

    sent = []

    def remote(src, dst, to, *key):
        i = copies(*key)
        return pltpu.make_async_remote_copy(
            src, dst, send_sems.at[i], recv_sems.at[i], device_id=to, device_id_type=MESH
        )

    def send(ref, to, *key, dst=None):
        copy = remote(ref, ref if dst is None else dst, to, *key)
        copy.start()
        sent.append(copy)

    def arrived(ref, to, *key):
        remote(ref, ref, to, *key).wait_recv()

    barrier = pltpu.get_barrier_semaphore()
    partners = [z_by(d, t) for d in (0, 1) for t in (1, 2)]
    partners += [*y_next, *x_next, sibling, after, before]
    for to in partners:
        pl.semaphore_signal(barrier, inc=1, device_id=to, device_id_type=MESH)
    pl.semaphore_wait(barrier, len(partners))

    def kv_at(u, d, s):
        return kv_weights.at[c, 0, u, slot(d, s)]

    def kv_pass(u, d, s, t):
        if s + t < half or (s + t == half and u == d):
            send(kv_at(u, d, s), z_by(d, t), "kv z", u, d, s + t, dst=kv_at(u, d, s + t))

    def qo_at(d, s):
        if s == half:
            return qo_weights.at[x, c, d, slot(d, s)]
        return qo_weights.at[x, c, :, slot(d, s)]

    def qo_pass(d, s, t):
        if s + t <= half:
            row = d if s + t == half else slice(None)
            src = qo_weights.at[x, c, row, slot(d, s)]
            send(src, z_by(d, t), "qo z", d, s + t, dst=qo_at(d, s + t))

    def normalize(first, last):
        def norm_step(i, carry):
            at = pl.ds(pl.multiple_of(i * NORM_ROWS, NORM_ROWS), NORM_ROWS)
            full = raw[at, :].astype(jnp.float32)
            centered = full - jnp.mean(full, axis=-1, keepdims=True)
            spread = jnp.mean(centered * centered, axis=-1, keepdims=True)
            scaled = centered * lax.rsqrt(spread + 1e-06)
            normed[at, :] = (scaled * (1.0 + mod[0:1, :]) + mod[1:2, :]).astype(jnp.bfloat16)
            return carry

        lax.fori_loop(first // NORM_ROWS, last // NORM_ROWS, norm_step, 0)

    def accumulate(u, first, places):
        lhs = jnp.concatenate([normed[:, column(row, at)] for row, at in places], axis=1)
        rhs = jnp.concatenate(
            [kv_weights[:, row, u, at].reshape(2 * ROWS, WIDTH) for row, at in places], axis=0
        )
        part = jnp.dot(lhs, rhs, preferred_element_type=jnp.float32)
        if first:
            acc[u] = part
        else:
            acc[u] += part

    def places_of(u, row, g):
        a, b = slots[g]
        arrived(kv_weights.at[1 - c, row, u, a:b], sibling, "kv s", u, row, g)
        return [(row, at) for at in range(a, b)]

    def stage_parts(u, g, d):
        odd = 2 * g + 1
        at = slot(d, odd)
        if odd + 1 < half:
            return [slice(at, at + 2)]
        return [slice(at, at + 1)] + ([slice(2 * half - 1, 2 * half)] if u == d else [])

    def across(u, g):
        for d in (0, 1):
            for i, at in enumerate(stage_parts(u, g, d)):
                ref, dst = kv_weights.at[c, 0, u, at], kv_weights.at[c, 1, u, at]
                send(ref, y_next[d], "kv y", u, g, d, i, dst=dst)

    def from_across(u, g):
        if g == 0:
            arrived(kv_weights.at[c, 1, u, 0], y_next[1 - u], "kv y own", u)
        for d in (0, 1):
            for i, at in enumerate(stage_parts(u, g, d)):
                arrived(kv_weights.at[c, 1, u, at], y_next[1 - d], "kv y", u, g, d, i)
        a, b = slots[g]
        send(kv_weights.at[c, 1, u, a:b], sibling, "kv s", u, 1, g)

    def qo_across_x(g):
        a, b = slots[g]
        for d in (0, 1):
            send(qo_weights.at[x, c, :, a:b], x_next[d], "qo x", g, d)

    def qo_relay_x(g):
        a, b = slots[g]
        for d in (0, 1):
            arrived(qo_weights.at[x_at[1 - d], c, :, a:b], x_next[1 - d], "qo x", g, d)
            send(qo_weights.at[x_at[1 - d], c, d, a:b], x_next[d], "qo r", g, d)

    def qo_to_core(g):
        a, b = slots[g]
        for d in (0, 1):
            arrived(qo_weights.at[x_far, c, d, a:b], x_next[1 - d], "qo r", g, d)
        send(qo_weights.at[:, c, :, a:b], sibling, "qo s", g)

    def qo_arrive(g):
        even = 2 * g + 2
        for d in (0, 1):
            arrived(qo_at(d, even), z_by(1 - d, 2), "qo z", d, even)
            for t in (2, 1):
                qo_pass(d, even, t)
        for d in (0, 1):
            arrived(qo_at(d, even - 1), z_by(1 - d, 1), "qo z", d, even - 1)
        qo_across_x(g)

    for u in (KEY, VALUE):
        loads[u].wait()
        for t in (2, 1):
            for d in (0, 1):
                kv_pass(u, d, 0, t)
        ref, dst = kv_weights.at[c, 0, u, 0], kv_weights.at[c, 1, u, 0]
        send(ref, y_next[u], "kv y own", u, dst=dst)
    loads[2].wait()
    loads[3].wait()
    send(qo_weights.at[x, c, 0, 0], y_next[0], "qo y", dst=qo_weights.at[x, c, 1, 0])
    loads[4].wait()
    loads[5].wait()
    loads[6].wait()
    normalize(0, BORDER)
    arrived(qo_weights.at[x, c, 1, 0], y_next[1], "qo y")
    for t in (2, 1):
        for d in (0, 1):
            qo_pass(d, 0, t)

    for g in range(stages):
        even = 2 * g + 2
        a, b = slots[g]
        for u in (KEY, VALUE):
            both = (0, 1) if even < half else (u,)
            for d in both:
                arrived(kv_at(u, d, even), z_by(1 - d, 2), "kv z", u, d, even)
                kv_pass(u, d, even, 2)
            for d in (0, 1):
                kv_pass(u, d, even, 1)
            for d in (0, 1):
                arrived(kv_at(u, d, even - 1), z_by(1 - d, 1), "kv z", u, d, even - 1)
            across(u, g)
            send(kv_weights.at[c, 0, u, a:b], sibling, "kv s", u, 0, g)
        if g == 0:
            normalize(BORDER, rows)
        else:
            for u in (KEY, VALUE):
                from_across(u, g - 1)
            qo_arrive(g - 1)
            if g > 1:
                qo_relay_x(g - 2)
            for u in (KEY, VALUE):
                places = places_of(u, 0, g - 1)
                if g > 1:
                    places += places_of(u, 1, g - 2)
                accumulate(u, g == 1, places)
    last = stages - 1
    for u in (KEY, VALUE):
        places = places_of(u, 0, last)
        if last > 0:
            places += places_of(u, 1, last - 1)
        accumulate(u, last == 0, places)
    for u in (KEY, VALUE):
        from_across(u, last)
    for u, name in ((KEY, "keys"), (VALUE, "values")):
        accumulate(u, False, places_of(u, 1, last))
        if u == KEY:
            local_rows = head_norm(acc[KEY], gain[1:2, :])
        else:
            local_rows = acc[VALUE].astype(jnp.bfloat16)
        held = keys if u == KEY else values
        held[BORDER : BORDER + rows, :] = local_rows
        ends = held.at[BORDER + rows : 2 * BORDER + rows]
        send(held.at[BORDER : 2 * BORDER], before, name + " head", dst=ends)
        send(held.at[rows : rows + BORDER], after, name + " tail", dst=held.at[0:BORDER])
        if u == KEY:
            qo_arrive(last)
            if last > 0:
                qo_relay_x(last - 1)

    qo_relay_x(last)
    for g in range(last):
        qo_to_core(g)

    def whole(row, at, which):
        return [qo_weights[q, core, row, at, which] for core in (0, 1) for q in range(PARTS)]

    def project(g_first, g_last, total):
        places = []
        for g in range(g_first, g_last):
            a, b = slots[g]
            arrived(qo_weights.at[:, 1 - c, :, a:b], sibling, "qo s", g)
            places += [(row, at) for row in (0, 1) for at in range(a, b)]
        for i in range(0, len(places), 6):
            group = places[i : i + 6]
            lhs = jnp.concatenate([normed[:, column(row, at)] for row, at in group], axis=1)
            rhs = jnp.concatenate([p for row, at in group for p in whole(row, at, QUERY)], axis=0)
            total = total + jnp.dot(lhs, rhs, preferred_element_type=jnp.float32)
        return total

    everything = [(row, at) for row in (0, 1) for at in range(n)]
    total = project(0, last, jnp.zeros((rows, WIDTH), jnp.float32))
    qo_to_core(last)
    total = project(last, stages, total)
    query[...] = head_norm(total, gain[0:1, :])

    scale = 1.0 / math.sqrt(HEAD_DIM)

    def raised_of(tile, head, start, count):
        cols = slice(head * HEAD_DIM, (head + 1) * HEAD_DIM)
        q = query[tile * TILE : (tile + 1) * TILE, cols]
        k = keys[start : start + count, cols]
        score = lax.dot_general(
            q, k, (((1,), (1,)), ((), ())), preferred_element_type=jnp.float32
        )
        return jnp.exp(score * scale)

    def mixed_values(share, head, start, count):
        v = values[start : start + count, head * HEAD_DIM : (head + 1) * HEAD_DIM]
        return jnp.dot(share, v, preferred_element_type=jnp.float32)

    for tile in range(tiles):
        for head in range(HEADS):
            raised = raised_of(tile, head, BORDER, rows)
            low = jnp.sum(raised, axis=-1, keepdims=True)
            bottom[tile, head] = jnp.broadcast_to(low, (TILE, HEAD_DIM))
            top[tile, head] = mixed_values(raised.astype(jnp.bfloat16), head, BORDER, rows)

    for row, at in everything:
        out_rows[column(row, at), :] = jnp.concatenate(whole(row, at, OUT), axis=0)

    def wait_border(held, name):
        arrived(held.at[0:BORDER], before, name + " tail")
        arrived(held.at[BORDER + rows : 2 * BORDER + rows], after, name + " head")

    def far_parts(tile):
        first, end = tile * TILE, (tile + 5) * TILE
        found, at = [], 0
        for start, stop, weight in (
            (first, BORDER, has_before),
            (BORDER + rows, end, has_after),
        ):
            if stop > start:
                found.append((start, stop - start, at, weight))
                at += stop - start
        return found

    has_before = jnp.where(frame > 0, 1.0, 0.0)
    has_after = jnp.where(frame < nx * nyh - 1, 1.0, 0.0)
    wait_border(keys, "keys")
    for tile in range(tiles):
        for head in range(HEADS):
            for start, count, at, weight in far_parts(tile):
                raised = raised_of(tile, head, start, count) * weight
                low = jnp.sum(raised, axis=-1, keepdims=True)
                bottom[tile, head] += jnp.broadcast_to(low, (TILE, HEAD_DIM))
                shares[tile, head, :, at : at + count] = raised.astype(jnp.bfloat16)
    wait_border(values, "values")
    for tile in range(tiles):
        done = []
        for head in range(HEADS):
            high = top[tile, head]
            for start, count, at, _ in far_parts(tile):
                share = shares[tile, head, :, at : at + count]
                high = high + mixed_values(share, head, start, count)
            done.append((high / bottom[tile, head]).astype(jnp.bfloat16))
        attended[tile * TILE : (tile + 1) * TILE, :] = jnp.concatenate(done, axis=1)

    for copy in sent:
        copy.wait_send()


def on_device(sizes, frames, modulation, w_qkv, qk_gain, w_out):
    n = sizes[0]
    rows, features = frames.shape[1:]
    anywhere = pl.BlockSpec(memory_space=pl.ANY)
    attended, out_rows = pl.pallas_call(
        functools.partial(kernel, sizes, Counter()),
        out_shape=(
            pltpu.VMEM((rows, WIDTH), jnp.bfloat16),
            pltpu.VMEM((features, WIDTH), jnp.bfloat16),
        ),
        in_specs=[anywhere] * 5,
        out_specs=(pl.BlockSpec(memory_space=pltpu.VMEM),) * 2,
        scratch_shapes=[
            pltpu.VMEM((2, 2, 2, n, ROWS, WIDTH), jnp.bfloat16),
            pltpu.VMEM((PARTS, 2, 2, n, 2, PIECE, WIDTH), jnp.bfloat16),
            pltpu.VMEM((rows, features), jnp.bfloat16),
            pltpu.VMEM((rows, features), jnp.bfloat16),
            pltpu.VMEM((2, features), jnp.float32),
            pltpu.VMEM((2, HEAD_DIM), jnp.float32),
            pltpu.VMEM((2, rows, WIDTH), jnp.float32),
            pltpu.VMEM((rows + 2 * BORDER, WIDTH), jnp.bfloat16),
            pltpu.VMEM((rows + 2 * BORDER, WIDTH), jnp.bfloat16),
            pltpu.VMEM((rows, WIDTH), jnp.bfloat16),
            pltpu.VMEM((rows // TILE, HEADS, TILE, HEAD_DIM), jnp.float32),
            pltpu.VMEM((rows // TILE, HEADS, TILE, HEAD_DIM), jnp.float32),
            pltpu.VMEM((rows // TILE, HEADS, TILE, BORDER), jnp.bfloat16),
            pltpu.SemaphoreType.DMA((7,)),
            pltpu.SemaphoreType.DMA((112,)),
            pltpu.SemaphoreType.DMA((112,)),
        ],
        compiler_params=pltpu.CompilerParams(collective_id=0, has_side_effects=True),
    )(frames[0], modulation[0], w_qkv, qk_gain, jnp.transpose(w_out))
    mixed = lax.dot_general(
        attended, out_rows, (((1,), (1,)), ((), ())), preferred_element_type=jnp.float32
    )
    return mixed.astype(jnp.bfloat16)[None]


def solution(mesh, n=12, nx=4, nyh=4):
    finer = Mesh(mesh.devices.reshape(2, n, 2, nx, nyh), AXES)
    fsdp, frame = ("yl", "z", "c"), ("x", "yh")
    placed = (P(fsdp, frame, None), P(fsdp, None, None), P(fsdp, None), P(), P(None, fsdp))
    return jax.shard_map(
        functools.partial(on_device, (n, nx, nyh)),
        mesh=finer,
        in_specs=placed,
        out_specs=P(fsdp, frame, None),
        check_vma=False,
    )
```

time: 64 us -> 62.4 us (0.975); the launches traced: 63.1 us -> 62.2 us
  local copies, waits for them, and re-layouts: 3.22 us -> 0 us
  matrix products: 0 us -> 2.22 us
    unnamed x1 -> x0, local copies, waits for them, and re-layouts: 3.22 us -> none
    dot_general x0 -> x1, matrix products: none -> 2.22 us  [on_device(): lax.dot_general(attended, out_rows, (((1,), (1,)), ((), ())), preferred_e...]
where the time goes in v3:
time: 62.4 us; the launch traced here: 62.2 us
  Pallas kernels  60 us (96%)
  matrix products  2.22 us (4%)
    pallas_call x1, Pallas kernels, on_device(): pl.pallas_call(functools.partial(kernel, sizes, Counter()), out_shape=(pl...  60 us
    dot_general x1, matrix products, on_device(): lax.dot_general(attended, out_rows, (((1,), (1,)), ((), ())), preferred_e...  2.22 us

profile of v3, /device:TPU:1, one launch (start us, length us, event | category | flops | bytes accessed | tf_op | source)
XLA Modules:
  0.0 62.2 jit_solution(13993904148510132125)
XLA Ops:
  0.0 60.0 %shard_map.55 = (bf16[384,256]{1,0:T(8,128)(2,1)S(1)}, bf16[3072,256]{1,0:T(8,128)(2,1)S(1)}) custom-call(bf16[384,3072]{1,0:T(8,128)(2,1)} %bitcast.7, f32[2,3072]{1,0:T(2,128)} %bitcast.9, bf16[64,768]{1,0:T(8,128)(2,1)} %w_qkv.1, f32[2,128]{1,0:T(2,128)} %qk_gain.1, bf16[64,256]{1,0:T(8,128)(2,1)} %bitcast.8), custom_call_target="tpu_custom_call" | custom-call | tf_op jit(solution)/shard_map/pallas_call | solution.py:423
  60.0 2.2 %fusion = bf16[1,384,3072]{2,1,0:T(8,128)(2,1)} fusion(bf16[384,256]{1,0:T(8,128)(2,1)S(1)} %get-tuple-element.7, bf16[3072,256]{1,0:T(8,128)(2,1)S(1)} %get-tuple-element.8), kind=kOutput, calls=%fused_computation.1 | convolution fusion | flops 605159424 | bytes 4128768 | tf_op jit(solution)/shard_map/dot_general | solution.py:451

commit v4 on v3

--- a/solution.py
+++ b/solution.py
@@ -308,6 +308,9 @@
         accumulate(u, last == 0, places)
     for u in (KEY, VALUE):
         from_across(u, last)
+    qo_arrive(last)
+    if last > 0:
+        qo_relay_x(last - 1)
     for u, name in ((KEY, "keys"), (VALUE, "values")):
         accumulate(u, False, places_of(u, 1, last))
         if u == KEY:
@@ -319,10 +322,6 @@
         ends = held.at[BORDER + rows : 2 * BORDER + rows]
         send(held.at[BORDER : 2 * BORDER], before, name + " head", dst=ends)
         send(held.at[rows : rows + BORDER], after, name + " tail", dst=held.at[0:BORDER])
-        if u == KEY:
-            qo_arrive(last)
-            if last > 0:
-                qo_relay_x(last - 1)
 
     qo_relay_x(last)
     for g in range(last):

time: 62.4 us -> 59.7 us (0.957)
  Pallas kernels: 60 us -> 57.4 us
    pallas_call x1, Pallas kernels: 60 us -> 57.4 us  [on_device(): pl.pallas_call(functools.partial(kernel, sizes, Counter()), out_shape=(pl...]
where the time goes in v4:
time: 59.7 us; the launch traced here: 59.6 us
  Pallas kernels  57.4 us (96%)
  matrix products  2.22 us (4%)
    pallas_call x1, Pallas kernels, on_device(): pl.pallas_call(functools.partial(kernel, sizes, Counter()), out_shape=(pl...  57.4 us
    dot_general x1, matrix products, on_device(): lax.dot_general(attended, out_rows, (((1,), (1,)), ((), ())), preferred_e...  2.22 us

profile of v4, /device:TPU:1, one launch (start us, length us, event | category | flops | bytes accessed | tf_op | source)
XLA Modules:
  0.0 59.6 jit_solution(4973917695003544999)
XLA Ops:
  0.0 57.4 %shard_map.55 = (bf16[384,256]{1,0:T(8,128)(2,1)S(1)}, bf16[3072,256]{1,0:T(8,128)(2,1)S(1)}) custom-call(bf16[384,3072]{1,0:T(8,128)(2,1)} %bitcast.7, f32[2,3072]{1,0:T(2,128)} %bitcast.9, bf16[64,768]{1,0:T(8,128)(2,1)} %w_qkv.1, f32[2,128]{1,0:T(2,128)} %qk_gain.1, bf16[64,256]{1,0:T(8,128)(2,1)} %bitcast.8), custom_call_target="tpu_custom_call" | custom-call | tf_op jit(solution)/shard_map/pallas_call | solution.py:422
  57.4 2.2 %fusion = bf16[1,384,3072]{2,1,0:T(8,128)(2,1)} fusion(bf16[384,256]{1,0:T(8,128)(2,1)S(1)} %get-tuple-element.7, bf16[3072,256]{1,0:T(8,128)(2,1)S(1)} %get-tuple-element.8), kind=kOutput, calls=%fused_computation.1 | convolution fusion | flops 605159424 | bytes 4128768 | tf_op jit(solution)/shard_map/dot_general | solution.py:450
